TPU v7x, 256 devices: a whole 4x4x8 slice. The times are simulated.
256 devices in a mesh: row: 16 (over z_lo, x, core), col: 16 (over z_hi, y).
Axes of the slice: x: 4, y: 4, z: 8 (z_hi: 4, z_lo: 2; z = z_hi * 2 + z_lo), core: 2. Of those that a mesh axis runs over, the one named last changes fastest.
Arguments:
- blocks_inverse: bfloat16 [12288, 12288], P('row', 'col'), as said below
- factor_rows: bfloat16 [2, 6144, 256], P(None, 'row'), may hold values from -0.15234375 to 0.15234375
- block_lists: int32 [2, 48], replicated, may hold values from 0 to 95, as said below
- diag_inverse: float32 [2, 256, 256], replicated, as said below
Outputs:
- column_inverse: float32 [2, 12288, 256], P(None, 'row')
- mirror_inverse: float32 [2, 256, 12288], P(None, None, 'col')
- diagonal_inverse: float32 [2, 256, 256], replicated
Inputs may be any that keep to these rules, and one draw needn't show every extreme that they name: blocks_inverse is exactly symmetric and positive definite. block_lists[s, m] is 2 * m or 2 * m + 1. diag_inverse[s] is symmetric.
All inputs are finite; a program needn't handle non-finite values.
Results may differ from a plain program's by a relative error of at most 0.0003.
Values may be sent and summed in bfloat16 or wider, within the bound.
A program may use at most 64 MiB of HBM per device.

v0:
```python
import jax
import jax.numpy as jnp
from jax import lax
from jax.sharding import PartitionSpec as P

BS = 128


def broadcast(x, axis, root):
    mine = lax.axis_index(axis) == root
    return lax.psum(jnp.where(mine, x, jnp.zeros_like(x)), axis)


def pair_bits(block_lists, first_block, block_count):
    local_lists = lax.dynamic_slice_in_dim(block_lists, first_block // 2, block_count // 2, 1)
    pair_first = 2 * (first_block // 2 + jnp.arange(block_count // 2, dtype=jnp.int32))
    return local_lists - pair_first[None, :]


def expand_pairs(packed, bits):
    sup_count = packed.shape[0]
    feature_count = packed.shape[2]
    pairs = bits.shape[1]
    grouped = packed.reshape(sup_count, pairs, 1, BS, feature_count)
    which = (
        bits[:, :, None, None, None] == jnp.arange(2, dtype=jnp.int32)[None, None, :, None, None]
    )
    dense = jnp.where(which, grouped, jnp.zeros((), packed.dtype))
    return dense.reshape(sup_count, pairs * 2 * BS, feature_count)


def compact_pairs(dense, bits):
    sup_count = dense.shape[0]
    feature_count = dense.shape[2]
    pairs = bits.shape[1]
    grouped = dense.reshape(sup_count, pairs, 2, BS, feature_count)
    chosen = jnp.where(bits[:, :, None, None] == 0, grouped[:, :, 0], grouped[:, :, 1])
    return chosen.reshape(sup_count, pairs * BS, feature_count)


def multiply_each(matrix, stacked):
    results = []
    for sup_index in range(stacked.shape[0]):
        results.append(
            jnp.dot(matrix, stacked[sup_index].astype(jnp.float32), precision=lax.Precision.HIGHEST)
        )
    return jnp.stack(results)


def local(blocks_inverse, factor_rows, block_lists, diag_inverse):
    row_index = lax.axis_index("row")
    col_index = lax.axis_index("col")
    row_blocks = blocks_inverse.shape[0] // BS
    col_blocks = blocks_inverse.shape[1] // BS
    row_bits = pair_bits(block_lists, row_index * row_blocks, row_blocks)
    col_bits = pair_bits(block_lists, col_index * col_blocks, col_blocks)
    packed_length = col_blocks // 2 * BS
    root_row = col_index * col_blocks // row_blocks
    gathered = lax.all_gather(factor_rows, "row", axis=1, tiled=True)
    column_packed = lax.dynamic_slice_in_dim(gathered, col_index * packed_length, packed_length, 1)
    column_dense = expand_pairs(column_packed, col_bits)
    blocks_wide = blocks_inverse.astype(jnp.float32)
    products = multiply_each(blocks_wide, column_dense)
    listed_products = compact_pairs(products, row_bits)
    diagonal_terms = jnp.einsum(
        "srw,srv->swv",
        factor_rows.astype(jnp.float32),
        listed_products,
        precision=lax.Precision.HIGHEST,
    )
    diagonal_inverse = diag_inverse + lax.psum(diagonal_terms, ("row", "col"))
    row_total = lax.psum(listed_products, "col")
    column_inverse = -expand_pairs(row_total, row_bits)
    mirror_total = broadcast(row_total, "row", root_row)
    mirror_inverse = jnp.transpose(-expand_pairs(mirror_total, col_bits), (0, 2, 1))
    return (column_inverse, mirror_inverse, diagonal_inverse)


def solution(mesh):
    return jax.shard_map(
        local,
        mesh=mesh,
        in_specs=(P("row", "col"), P(None, "row", None), P(), P()),
        out_specs=(P(None, "row", None), P(None, None, "col"), P()),
        check_vma=False,
    )
```

profile of v0, /device:TPU:1, one launch (start us, length us, event | category | flops | bytes accessed | tf_op | source)
XLA Modules:
  0.0 641.8 jit_solution(4474671392308871341)
XLA Ops:
  8.0 0.8 broadcast_compare_fusion
  8.8 0.8 dynamic-slice_subtract_fusion
  9.6 49.3 %all-gather.2.cloned.1.call-done = bf16[2,6144,256]{2,1,0:T(8,128)(2,1)} async-done(((bf16[2,384,256]{2,1,0:T(8,128)(2,1)}), bf16[2,6144,256]{2,1,0:T(8,128)(2,1)}) %all-gather.2.cloned.1.call-update) | async-done | bytes 6291472 | tf_op jit(solution)/shard_map/all_gather | solution.py:59
  59.0 1.0 constant_dynamic-slice_fusion
  60.1 0.8 fusion.1
  61.9 1.5 convolution_bitcast_fusion
  64.4 1.2 fusion
  65.6 1.0 copy.11
  66.6 1.0 copy.10
  67.8 3.0 convolution_bitcast_fusion.2
  72.3 160.2 %all-reduce.4.cloned.1.call-done = f32[2,384,256]{2,1,0:T(8,128)} async-done(((f32[2,384,256]{2,1,0:T(8,128)}), f32[2,384,256]{2,1,0:T(8,128)}) %all-reduce.4.cloned.1.call-update) | async-done | bytes 786448 | tf_op jit(solution)/shard_map/psum | solution.py:72
  232.5 0.9 broadcast_select_fusion.1
  234.0 267.5 %all-reduce.8.cloned.1.call-done = f32[2,256,256]{1,2,0:T(8,128)} async-done(((f32[2,256,256]{1,2,0:T(8,128)}), f32[2,256,256]{1,2,0:T(8,128)}) %all-reduce.8.cloned.1.call-update) | async-done | bytes 524304 | tf_op jit(solution)/shard_map/psum | solution.py:71
  501.5 1.1 add.48
  502.6 1.0 copy.17
  504.0 1.7 broadcast_in_dim.104
  505.7 2.5 broadcast_in_dim.105
  508.2 1.3 select_negate_fusion
  509.5 3.0 copy.16
  512.5 115.7 %all-reduce.6.cloned.1.call-done = f32[2,3,128,256]{3,2,1,0:T(8,128)} async-done(((f32[2,3,128,256]{3,2,1,0:T(8,128)}), f32[2,3,128,256]{3,2,1,0:T(8,128)}) %all-reduce.6.cloned.1.call-update) | async-done | bytes 786448 | tf_op jit(solution)/shard_map/psum | solution.py:11
  628.2 1.5 copy.13
  629.8 1.7 broadcast_in_dim.112
  631.4 2.5 broadcast_in_dim.113
  634.0 1.3 negate_bitcast_fusion
  (35 shorter events, 5.4 us)
Async XLA Ops:
  7.2 53.8 %copy-start = (bf16[768,768]{1,0:T(8,128)(2,1)S(1)}, bf16[768,768]{1,0:T(8,128)(2,1)}, u32[]{:S(2)}) copy-start(bf16[768,768]{1,0:T(8,128)(2,1)} %param.4) | copy-start | bytes 3538948
  7.2 51.8 %all-gather.2.cloned.1.call-start = ((), (), s32[]{:S(2)}) async-start(), calls=%async_computation | async-start | bytes 6684672 | tf_op jit(solution)/shard_map/all_gather | solution.py:59
  67.8 3.0 copy-start.1
  70.8 161.8 %all-reduce.4.cloned.1.call-start = ((), (), s32[]{:S(2)}) async-start(), calls=%async_computation.1 | async-start | bytes 1572864 | tf_op jit(solution)/shard_map/psum | solution.py:72
  71.5 162.3 %copy-start.3 = (f32[2,256,256]{2,1,0:T(8,128)S(1)}, f32[2,256,256]{2,1,0:T(8,128)}, u32[]{:S(2)}) copy-start(f32[2,256,256]{2,1,0:T(8,128)} %param.7) | copy-start | bytes 1572868
  71.5 430.0 %all-reduce.8.cloned.1.call-start = ((), (), s32[]{:S(2)}) async-start(), calls=%async_computation.3 | async-start | bytes 1048576 | tf_op jit(solution)/shard_map/psum | solution.py:71
  72.2 556.0 %all-reduce.6.cloned.1.call-start = ((), (), s32[]{:S(2)}) async-start(), calls=%async_computation.2 | async-start | bytes 1572864 | tf_op jit(solution)/shard_map/psum | solution.py:11
  234.0 269.6 %copy-start.2 = (f32[2,384,256]{2,1,0:T(8,128)S(1)}, f32[2,384,256]{2,1,0:T(8,128)}, u32[]{:S(2)}) copy-start(f32[2,384,256]{2,1,0:T(8,128)} %all-reduce.4.cloned.1.call-done) | copy-start | bytes 2359300
Sparse Core Ops, SparseCore 0:
  9.8 49.1 all-gather.1
  74.8 157.7 all-reduce.3
  238.6 262.8 all-reduce.7
  504.0 124.2 all-reduce.5
where the time goes:
time: 642 us
  waiting for transfers between devices  595 us (93%)
  local copies, waits for them, and re-layouts  21.3 us (3%)
  between operations  14 us (2%)
  other arithmetic  6.57 us (1%)
    psum x1, waiting for transfers between devices, local(): diagonal_inverse = diag_inverse + lax.psum(diagonal_terms, ('row', 'col'))  268 us
    psum x1, waiting for transfers between devices, local(): row_total = lax.psum(listed_products, 'col')  160 us
    psum x1, waiting for transfers between devices, broadcast(): return lax.psum(jnp.where(mine, x, jnp.zeros_like(x)), axis)  116 us
    all_gather x1, waiting for transfers between devices, local(): gathered = lax.all_gather(factor_rows, 'row', axis=1, tiled=True)  49.3 us
  transfers between devices with their start and end apart: 4, of which 4 were waited for; matrix products, arithmetic and copies ran while one was open for 2% of the time, Pallas kernels for 0%

commit v1 on v0

--- a/solution.py
+++ b/solution.py
@@ -4,6 +4,11 @@
 from jax.sharding import PartitionSpec as P
 
 BS = 128
+
+
+def by_each_axis(value, first, second):
+    partial = lax.psum(value, first)
+    return lax.psum(partial, second)
 
 
 def broadcast(x, axis, root):
@@ -68,7 +73,7 @@
         listed_products,
         precision=lax.Precision.HIGHEST,
     )
-    diagonal_inverse = diag_inverse + lax.psum(diagonal_terms, ("row", "col"))
+    diagonal_inverse = diag_inverse + by_each_axis(diagonal_terms, "row", "col")
     row_total = lax.psum(listed_products, "col")
     column_inverse = -expand_pairs(row_total, row_bits)
     mirror_total = broadcast(row_total, "row", root_row)

time: 642 us -> 509 us (0.79)
  waiting for transfers between devices: 595 us -> 464 us
    psum x1, waiting for transfers between devices: 268 us -> 124 us  [by_each_axis(): partial = lax.psum(value, first)]
    psum x1, waiting for transfers between devices: 116 us -> 124 us  [broadcast(): return lax.psum(jnp.where(mine, x, jnp.zeros_like(x)), axis)]
where the time goes in v1:
time: 509 us
  waiting for transfers between devices  464 us (91%)
  local copies, waits for them, and re-layouts  22.1 us (4%)
  between operations  14 us (3%)
  other arithmetic  5.54 us (1%)
    psum x1, waiting for transfers between devices, local(): row_total = lax.psum(listed_products, 'col')  166 us
    psum x1, waiting for transfers between devices, broadcast(): return lax.psum(jnp.where(mine, x, jnp.zeros_like(x)), axis)  124 us
    psum x1, waiting for transfers between devices, by_each_axis(): partial = lax.psum(value, first)  124 us
    all_gather x1, waiting for transfers between devices, local(): gathered = lax.all_gather(factor_rows, 'row', axis=1, tiled=True)  49.3 us
  transfers between devices with their start and end apart: 4, of which 4 were waited for; matrix products, arithmetic and copies ran while one was open for 2% of the time, Pallas kernels for 0%

profile of v1, /device:TPU:1, one launch (start us, length us, event | category | flops | bytes accessed | tf_op | source)
XLA Modules:
  0.0 509.0 jit_solution(12133648193900890622)
XLA Ops:
  8.0 0.8 broadcast_compare_fusion
  8.9 0.8 dynamic-slice_subtract_fusion
  9.7 49.3 %all-gather.2.cloned.1.call-done = bf16[2,6144,256]{2,1,0:T(8,128)(2,1)} async-done(((bf16[2,384,256]{2,1,0:T(8,128)(2,1)}), bf16[2,6144,256]{2,1,0:T(8,128)(2,1)}) %all-gather.2.cloned.1.call-update) | async-done | bytes 6291472 | tf_op jit(solution)/shard_map/all_gather | solution.py:64
  59.0 1.0 constant_dynamic-slice_fusion
  60.1 0.8 fusion.1
  61.9 1.5 convolution_bitcast_fusion
  64.4 1.2 fusion
  65.6 1.0 copy.11
  66.6 1.0 copy.10
  67.8 0.8 copy-done.3
  68.6 1.7 convolution_bitcast_fusion.2
  70.4 123.6 %all-reduce.7.cloned.1.call-done = f32[2,256,256]{1,2,0:T(8,128)} async-done(((f32[2,256,256]{1,2,0:T(8,128)}), f32[2,256,256]{1,2,0:T(8,128)}) %all-reduce.7.cloned.1.call-update) | async-done | bytes 524304 | tf_op jit(solution)/shard_map/psum | solution.py:10
  194.1 166.2 %all-reduce.9.cloned.1.call-done = (f32[2,384,256]{2,1,0:T(8,128)}, f32[2,256,256]{1,2,0:T(8,128)}) async-done(((f32[2,384,256]{2,1,0:T(8,128)}, f32[2,256,256]{1,2,0:T(8,128)}), (f32[2,384,256]{2,1,0:T(8,128)}, f32[2,256,256]{1,2,0:T(8,128)})) %all-reduce.9.cloned.1.call-update) | async-done | bytes 1310736 | tf_op jit(solution)/shard_map/psum | solution.py:77
  360.3 0.9 broadcast_select_fusion.1
  361.8 1.0 copy.17
  363.3 1.7 broadcast_in_dim.104
  365.0 2.5 broadcast_in_dim.105
  367.5 1.3 select_negate_fusion
  368.8 3.0 copy.16
  371.8 123.7 %all-reduce.5.cloned.1.call-done = f32[2,3,128,256]{3,2,1,0:T(8,128)} async-done(((f32[2,3,128,256]{3,2,1,0:T(8,128)}), f32[2,3,128,256]{3,2,1,0:T(8,128)}) %all-reduce.5.cloned.1.call-update) | async-done | bytes 786448 | tf_op jit(solution)/shard_map/psum | solution.py:16
  495.5 1.5 copy.13
  497.0 1.7 broadcast_in_dim.112
  498.7 2.5 broadcast_in_dim.113
  501.2 1.3 negate_bitcast_fusion
  (39 shorter events, 4.2 us)
Async XLA Ops:
  7.2 53.8 %copy-start = (bf16[768,768]{1,0:T(8,128)(2,1)S(1)}, bf16[768,768]{1,0:T(8,128)(2,1)}, u32[]{:S(2)}) copy-start(bf16[768,768]{1,0:T(8,128)(2,1)} %param.4) | copy-start | bytes 3538948
  7.2 51.8 %all-gather.2.cloned.1.call-start = ((), (), s32[]{:S(2)}) async-start(), calls=%async_computation | async-start | bytes 6684672 | tf_op jit(solution)/shard_map/all_gather | solution.py:64
  7.9 186.1 %all-reduce.7.cloned.1.call-start = ((), (), s32[]{:S(2)}) async-start(), calls=%async_computation.2 | async-start | bytes 1048576 | tf_op jit(solution)/shard_map/psum | solution.py:10
  67.6 1.0 copy-start.3
  68.6 125.3 %copy-start.1 = (f32[2,384,256]{2,1,0:T(8,128)}, f32[2,384,256]{2,1,0:T(8,128)S(1)}, u32[]{:S(2)}) copy-start(f32[2,384,256]{2,1,0:T(8,128)S(1)} %broadcast_select_fusion.2) | copy-start | bytes 2359300
  70.3 290.0 %all-reduce.9.cloned.1.call-start = ((), (), s32[]{:S(2)}) async-start(), calls=%async_computation.3 | async-start | bytes 2621440 | tf_op jit(solution)/shard_map/psum | solution.py:77
  194.0 167.6 %copy-start.5 = (f32[2,256,256]{2,1,0:T(8,128)S(1)}, f32[2,256,256]{2,1,0:T(8,128)}, u32[]{:S(2)}) copy-start(f32[2,256,256]{2,1,0:T(8,128)} %param.7) | copy-start | bytes 1572868
  194.0 301.5 %all-reduce.5.cloned.1.call-start = ((), (), s32[]{:S(2)}) async-start(), calls=%async_computation.1 | async-start | bytes 1572864 | tf_op jit(solution)/shard_map/psum | solution.py:16
  360.3 1.5 copy-start.4
  361.8 1.1 copy-start.2
Sparse Core Ops, SparseCore 0:
  9.8 49.1 all-gather.1
  70.4 123.4 all-reduce.6
  197.3 163.0 all-reduce.8
  362.8 132.6 all-reduce.4
